TPU v7x, 512 devices: a whole 4x4x16 slice. The times are simulated.
512 devices in a mesh: wide: 128 (over z, y, core), pair: 4 (over x).
Axes of the slice: x: 4, y: 4, z: 16, core: 2. Of those that a mesh axis runs over, the one named last changes fastest.
Arguments:
- three_center: bfloat16 [512, 8, 1024], P('wide'), may hold values from -0.3125 to 0.3125
- occ_green: bfloat16 [512, 128, 8, 8], P('wide', 'pair'), may hold values from -2 to 2
- virt_green: bfloat16 [512, 128, 8, 8], P('wide', 'pair'), may hold values from -2 to 2
- occ_column: int32 [512, 128], P('wide', 'pair'), may hold values from 0 to 511, as said below
- partner_live: int32 [512, 128], P('wide', 'pair'), may hold values 0 or 1
Outputs:
- response: float32 [128, 128], P('pair')
Inputs may be any that keep to these rules, and one draw needn't show every extreme that they name: `occ_column`: for each index of pair and each index w of wide, the slots of that group on the 4 atom blocks w * 4 to w * 4 + 3 name partner blocks k such that no value of k // 4 occurs more than 2 times, and some value occurs exactly 2 times.
All inputs are finite; a program needn't handle non-finite values. No bound on the sum of `partner_live` on one device may be relied on, other than what follows from the above.
Results may differ from a plain program's by a relative error of at most 0.004.
Values may be sent and summed in bfloat16 or wider, within the bound.
A program may use at most 64 MiB of HBM per device.

v0:
```python
import jax
import jax.numpy as jnp
from jax import lax
from jax.sharding import PartitionSpec as P

CAP = 2


def apply_virtual(occupied, virt_blocks, block_size):
    shaped = occupied.reshape(occupied.shape[:-1] + (block_size, -1))
    product = jnp.einsum(
        "...lnp,...ns->...lsp", shaped, virt_blocks, preferred_element_type=jnp.float32
    )
    return product.astype(jnp.bfloat16).reshape(occupied.shape)


def slot_ranks(owners):
    unit_count = owners.shape[-1]
    same_owner = owners[..., :, None] == owners[..., None, :]
    before = jnp.arange(unit_count)[None, :] < jnp.arange(unit_count)[:, None]
    return jnp.sum(same_owner & before, axis=-1)


def local(three_center, occ_green, virt_green, occ_column, partner_live):
    local_atoms, block_size, wide_row = three_center.shape
    aux_count = wide_row // block_size
    wide_count = lax.axis_size("wide")
    slot_total = wide_count * CAP
    unit_count = occ_green.shape[0] * occ_green.shape[1]
    listed = lax.all_gather(occ_column, "wide", axis=0, tiled=True).reshape(wide_count, unit_count)
    listed_owner = listed // local_atoms
    listed_rank = slot_ranks(listed_owner)
    to_here = listed_owner == lax.axis_index("wide")
    chosen = to_here[:, None, :] & (listed_rank[:, None, :] == jnp.arange(CAP)[None, :, None])
    slot_atom = jnp.sum(jnp.where(chosen, (listed % local_atoms)[:, None, :], 0), axis=2).reshape(
        slot_total
    )
    slot_used = jnp.any(chosen, axis=2).reshape(slot_total)
    occupied = jnp.einsum(
        "amnl,anx->amlx", occ_green, three_center, preferred_element_type=jnp.float32
    )
    occupied = occupied * partner_live.astype(jnp.float32)[:, :, None, None]
    occupied = occupied.astype(jnp.bfloat16).reshape(unit_count, block_size, wide_row)
    owners = (occ_column // local_atoms).reshape(unit_count)
    position = owners * CAP + slot_ranks(owners)
    virt_units = virt_green.reshape(unit_count, block_size, block_size)
    own_rows = three_center.astype(jnp.float32).reshape(-1, aux_count)
    both = apply_virtual(occupied, virt_units, block_size)
    outgoing = jnp.zeros((slot_total, block_size, wide_row), jnp.bfloat16).at[position].set(both)
    arrived = lax.all_to_all(
        outgoing.reshape(wide_count, CAP, block_size, wide_row),
        "wide",
        split_axis=0,
        concat_axis=0,
        tiled=True,
    )
    routing = (
        (slot_atom[None, :] == jnp.arange(local_atoms)[:, None]) & slot_used[None, :]
    ).astype(jnp.bfloat16)
    partner_sum = jnp.dot(
        routing, arrived.reshape(slot_total, -1), preferred_element_type=jnp.float32
    )
    partner_rows = partner_sum.reshape(-1, aux_count)
    response_part = lax.dot_general(
        partner_rows,
        own_rows,
        (((0,), (0,)), ((), ())),
        precision=lax.Precision.HIGHEST,
        preferred_element_type=jnp.float32,
    )
    total = lax.psum(response_part, ("wide", "pair"))
    row_count = aux_count // lax.axis_size("pair")
    result = lax.dynamic_slice_in_dim(total, lax.axis_index("pair") * row_count, row_count, 0)
    return result


def solution(mesh):
    placed = (
        P("wide", None, None),
        P("wide", "pair", None, None),
        P("wide", "pair", None, None),
        P("wide", "pair"),
        P("wide", "pair"),
    )
    return jax.shard_map(
        local, mesh=mesh, in_specs=placed, out_specs=P("pair", None), check_vma=False
    )
```

profile of v0, /device:TPU:1, one launch (start us, length us, event | category | flops | bytes accessed | tf_op | source)
XLA Modules:
  0.0 793.3 jit_solution(15315771442357756404)
XLA Ops:
  6.5 0.7 broadcast_multiply_fusion
  7.2 0.1 mul.26
  7.3 0.1 eq.80
  7.4 0.2 convert_reduce_fusion.1
  7.6 1.1 copy.39
  8.7 1.1 copy.33
  9.8 0.7 convert_element_type.22
  10.5 1.5 multiply_convert_fusion
  12.0 2.0 convert_bitcast_fusion
  14.1 2.8 reshape.166
  16.9 2.5 broadcast_in_dim.12
  19.4 15.7 %scatter_fusion = bf16[256,8,1024]{2,1,0:T(8,128)(2,1)} fusion(bf16[256,8,1024]{2,1,0:T(8,128)(2,1)} %broadcast_in_dim.12, s32[128]{0:T(128)S(1)} %fusion.17, bf16[128,8,1024]{2,1,0:T(8,128)(2,1)S(1)} %reshape.166), kind=kCustom, calls=%fused_computation | custom fusion | bytes 6291968 | tf_op jit(solution)/shard_map/scatter | solution.py:49
  35.1 0.0 copy-start
  35.1 0.0 copy-start.1
  35.1 21.1 %all-to-all-start = ((bf16[128,2,8,1024]{3,2,1,0:T(8,128)(2,1)}), bf16[128,2,8,1024]{3,2,1,0:T(8,128)(2,1)}, u32[]{:S(2)}, u32[]{:S(2)}) async-start(bf16[128,2,8,1024]{3,2,1,0:T(8,128)(2,1)} %bitcast.58), calls=%async_computation | async-start | bytes 8388608 | tf_op jit(solution)/shard_map/all_to_all | solution.py:50
  56.3 0.0 all-reduce.2.cloned.1.call-start
  56.3 0.0 copy-done
  56.4 0.0 copy-done.1
  56.4 276.5 %all-gather = s32[128,4,32]{2,1,0:T(4,128)S(1)} all-gather(s32[1,4,32]{2,1,0:T(4,128)S(1)} %bitcast.62), channel_id=1, replica_groups=mesh['wide'=128,'pair'=4] {'wide'}, dimensions={0}, use_global_device_ids=true | all-gather | bytes 66048 | tf_op jit(solution)/shard_map/all_gather | solution.py:30
  332.9 0.1 copy.26
  333.1 0.1 copy.30
  333.2 0.1 broadcast_compare_fusion
  333.2 0.1 copy.28
  333.3 0.1 copy.27
  333.5 5.1 convert_reduce_fusion
  338.6 0.1 select_reduce_fusion
  338.7 0.1 copy.31
  338.8 0.1 eq.76
  339.0 0.1 fusion.5
  339.1 0.1 copy.32
  339.2 0.2 and.81
  339.4 0.0 all-to-all-done
  339.4 6.5 copy.41
  345.9 0.7 fusion.11
  346.6 0.1 reshape.160
  346.7 0.9 fusion.18
  347.6 0.0 all-reduce.2.cloned.1.call-update
  347.6 437.5 %all-reduce.2.cloned.1.call-done = f32[128,128]{1,0:T(8,128)} async-done(((f32[128,128]{1,0:T(8,128)}), f32[128,128]{1,0:T(8,128)}) %all-reduce.2.cloned.1.call-update) | async-done | bytes 65552 | tf_op jit(solution)/shard_map/psum | solution.py:71
  785.1 1.3 constant_dynamic-slice_fusion
  (4 shorter events, 0.1 us)
Async XLA Ops:
  35.1 21.2 %copy-start = (bf16[4,8,1024]{2,1,0:T(8,128)(2,1)S(1)}, bf16[4,8,1024]{2,1,0:T(8,128)(2,1)}, u32[]{:S(2)}) copy-start(bf16[4,8,1024]{2,1,0:T(8,128)(2,1)} %param.5) | copy-start | bytes 196612
  35.1 21.3 %copy-start.1 = (s32[4,32]{1,0:T(4,128)S(1)}, s32[4,32]{1,0:T(4,128)}, u32[]{:S(2)}) copy-start(s32[4,32]{1,0:T(4,128)} %param.8) | copy-start | bytes 1540
  35.1 304.2 %all-to-all-start = ((bf16[128,2,8,1024]{3,2,1,0:T(8,128)(2,1)}), bf16[128,2,8,1024]{3,2,1,0:T(8,128)(2,1)}, u32[]{:S(2)}, u32[]{:S(2)}) async-start(bf16[128,2,8,1024]{3,2,1,0:T(8,128)(2,1)} %bitcast.58), calls=%async_computation | async-start | bytes 8388608 | tf_op jit(solution)/shard_map/all_to_all | solution.py:50
  56.3 728.9 %all-reduce.2.cloned.1.call-start = ((), (), s32[]{:S(2)}) async-start(), calls=%async_computation.1 | async-start | bytes 131072 | tf_op jit(solution)/shard_map/psum | solution.py:71
Sparse Core Ops, SparseCore 0:
  347.7 437.3 all-reduce.1
where the time goes:
time: 794 us; the launch traced here: 793 us
  waiting for transfers between devices  438 us (55%)
  blocking collectives  277 us (35%)
  local copies, waits for them, and re-layouts  32.4 us (4%)
  starting transfers between devices  21.2 us (3%)
  between operations  13.6 us (2%)
    psum x1, waiting for transfers between devices, local(): total = lax.psum(response_part, ('wide', 'pair'))  438 us
    all_gather x1, blocking collectives, local(): lax.all_gather(occ_column, 'wide', axis=0, tiled=True)  277 us
    all_to_all x1, starting transfers between devices, local(): lax.all_to_all(outgoing.reshape(wide_count, CAP, block_size, wide_row), '...  21.1 us
  transfers between devices with their start and end apart: 2, of which 1 were waited for; matrix products, arithmetic and copies ran while one was open for 1% of the time, Pallas kernels for 0%

commit v1 on v0

--- a/solution.py
+++ b/solution.py
@@ -68,7 +68,7 @@
         precision=lax.Precision.HIGHEST,
         preferred_element_type=jnp.float32,
     )
-    total = lax.psum(response_part, ("wide", "pair"))
+    total = lax.psum(lax.psum(response_part, "wide"), "pair")
     row_count = aux_count // lax.axis_size("pair")
     result = lax.dynamic_slice_in_dim(total, lax.axis_index("pair") * row_count, row_count, 0)
     return result

time: 794 us -> 714 us (0.90)
  waiting for transfers between devices: 438 us -> 356 us
    psum x1 -> x2, waiting for transfers between devices: 438 us -> 356 us  [local(): total = lax.psum(lax.psum(response_part, 'wide'), 'pair')]
  transfers between devices with their start and end apart: 2 -> 3, of which waited for: 1 -> 2; matrix products, arithmetic and copies ran while one was open for 1% -> 1% of each run, Pallas kernels for 0% -> 0%
where the time goes in v1:
time: 714 us; the launch traced here: 712 us
  waiting for transfers between devices  356 us (50%)
  blocking collectives  277 us (39%)
  local copies, waits for them, and re-layouts  32.4 us (5%)
  starting transfers between devices  21.2 us (3%)
  between operations  13.6 us (2%)
    psum x2, waiting for transfers between devices, local(): total = lax.psum(lax.psum(response_part, 'wide'), 'pair')  356 us
    all_gather x1, blocking collectives, local(): lax.all_gather(occ_column, 'wide', axis=0, tiled=True)  277 us
    all_to_all x1, starting transfers between devices, local(): lax.all_to_all(outgoing.reshape(wide_count, CAP, block_size, wide_row), '...  21.1 us
    scatter x1, local copies, waits for them, and re-layouts, local(): jnp.zeros((slot_total, block_size, wide_row), jnp.bfloat16).at[position]  15.7 us
  transfers between devices with their start and end apart: 3, of which 2 were waited for; matrix products, arithmetic and copies ran while one was open for 1% of the time, Pallas kernels for 0%

profile of v1, /device:TPU:1, one launch (start us, length us, event | category | flops | bytes accessed | tf_op | source)
XLA Modules:
  0.0 711.9 jit_solution(1897298928600355254)
XLA Ops:
  6.5 0.7 broadcast_multiply_fusion
  7.2 0.1 mul.26
  7.3 0.1 eq.80
  7.4 0.2 convert_reduce_fusion.1
  7.6 1.1 copy.39
  8.7 1.1 copy.33
  9.8 0.7 convert_element_type.22
  10.5 1.5 multiply_convert_fusion
  12.0 2.0 convert_bitcast_fusion
  14.1 2.8 reshape.166
  16.9 2.5 broadcast_in_dim.12
  19.4 15.7 %scatter_fusion = bf16[256,8,1024]{2,1,0:T(8,128)(2,1)} fusion(bf16[256,8,1024]{2,1,0:T(8,128)(2,1)} %broadcast_in_dim.12, s32[128]{0:T(128)S(1)} %fusion.17, bf16[128,8,1024]{2,1,0:T(8,128)(2,1)S(1)} %reshape.166), kind=kCustom, calls=%fused_computation | custom fusion | bytes 6291968 | tf_op jit(solution)/shard_map/scatter | solution.py:49
  35.1 0.0 copy-start
  35.1 0.0 copy-start.1
  35.1 21.1 %all-to-all-start = ((bf16[128,2,8,1024]{3,2,1,0:T(8,128)(2,1)}), bf16[128,2,8,1024]{3,2,1,0:T(8,128)(2,1)}, u32[]{:S(2)}, u32[]{:S(2)}) async-start(bf16[128,2,8,1024]{3,2,1,0:T(8,128)(2,1)} %bitcast.58), calls=%async_computation | async-start | bytes 8388608 | tf_op jit(solution)/shard_map/all_to_all | solution.py:50
  56.3 0.0 all-reduce.3.cloned.1.call-start
  56.3 0.0 copy-done
  56.4 0.0 copy-done.1
  56.4 276.5 %all-gather = s32[128,4,32]{2,1,0:T(4,128)S(1)} all-gather(s32[1,4,32]{2,1,0:T(4,128)S(1)} %bitcast.62), channel_id=1, replica_groups=mesh['wide'=128,'pair'=4] {'wide'}, dimensions={0}, use_global_device_ids=true | all-gather | bytes 66048 | tf_op jit(solution)/shard_map/all_gather | solution.py:30
  332.9 0.1 copy.26
  333.1 0.1 copy.30
  333.2 0.1 broadcast_compare_fusion
  333.2 0.1 copy.28
  333.3 0.1 copy.27
  333.5 5.1 convert_reduce_fusion
  338.6 0.1 select_reduce_fusion
  338.7 0.1 copy.31
  338.8 0.1 eq.76
  339.0 0.1 fusion.5
  339.1 0.1 copy.32
  339.2 0.2 and.81
  339.4 0.0 all-to-all-done
  339.4 6.5 copy.41
  345.9 0.7 fusion.11
  346.6 0.1 reshape.160
  346.7 0.9 fusion.18
  347.6 0.0 all-reduce.3.cloned.1.call-update
  347.6 0.0 all-reduce.5.cloned.1.call-start
  347.6 307.2 %all-reduce.3.cloned.1.call-done = f32[128,128]{1,0:T(8,128)} async-done(((f32[128,128]{1,0:T(8,128)}), f32[128,128]{1,0:T(8,128)}) %all-reduce.3.cloned.1.call-update) | async-done | bytes 65552 | tf_op jit(solution)/shard_map/psum | solution.py:71
  654.8 0.0 all-reduce.5.cloned.1.call-update
  654.9 48.9 %all-reduce.5.cloned.1.call-done = f32[128,128]{1,0:T(8,128)} async-done(((f32[128,128]{1,0:T(8,128)}), f32[128,128]{1,0:T(8,128)}) %all-reduce.5.cloned.1.call-update) | async-done | bytes 65552 | tf_op jit(solution)/shard_map/psum | solution.py:71
  703.7 1.3 constant_dynamic-slice_fusion
  (4 shorter events, 0.1 us)
Async XLA Ops:
  35.1 21.2 %copy-start = (bf16[4,8,1024]{2,1,0:T(8,128)(2,1)S(1)}, bf16[4,8,1024]{2,1,0:T(8,128)(2,1)}, u32[]{:S(2)}) copy-start(bf16[4,8,1024]{2,1,0:T(8,128)(2,1)} %param.5) | copy-start | bytes 196612
  35.1 21.3 %copy-start.1 = (s32[4,32]{1,0:T(4,128)S(1)}, s32[4,32]{1,0:T(4,128)}, u32[]{:S(2)}) copy-start(s32[4,32]{1,0:T(4,128)} %param.8) | copy-start | bytes 1540
  35.1 304.2 %all-to-all-start = ((bf16[128,2,8,1024]{3,2,1,0:T(8,128)(2,1)}), bf16[128,2,8,1024]{3,2,1,0:T(8,128)(2,1)}, u32[]{:S(2)}, u32[]{:S(2)}) async-start(bf16[128,2,8,1024]{3,2,1,0:T(8,128)(2,1)} %bitcast.58), calls=%async_computation | async-start | bytes 8388608 | tf_op jit(solution)/shard_map/all_to_all | solution.py:50
  56.3 598.6 %all-reduce.3.cloned.1.call-start = ((), (), s32[]{:S(2)}) async-start(), calls=%async_computation.1 | async-start | bytes 131072 | tf_op jit(solution)/shard_map/psum | solution.py:71
  347.6 356.1 %all-reduce.5.cloned.1.call-start = ((), (), s32[]{:S(2)}) async-start(), calls=%async_computation.2 | async-start | bytes 131072 | tf_op jit(solution)/shard_map/psum | solution.py:71
Sparse Core Ops, SparseCore 0:
  347.7 307.0 all-reduce.2
  657.1 46.5 all-reduce.4

commit v2 on v0

--- a/solution.py
+++ b/solution.py
@@ -27,7 +27,9 @@
     wide_count = lax.axis_size("wide")
     slot_total = wide_count * CAP
     unit_count = occ_green.shape[0] * occ_green.shape[1]
-    listed = lax.all_gather(occ_column, "wide", axis=0, tiled=True).reshape(wide_count, unit_count)
+    listed = jnp.concatenate(
+        lax.all_to_all(jnp.stack([occ_column] * lax.axis_size("wide")), "wide", 0, 0), axis=0
+    ).reshape(wide_count, unit_count)
     listed_owner = listed // local_atoms
     listed_rank = slot_ranks(listed_owner)
     to_here = listed_owner == lax.axis_index("wide")

time: 794 us -> 713 us (0.90)
  blocking collectives: 277 us -> 0 us
  waiting for transfers between devices: 438 us -> 613 us
  starting transfers between devices: 21.2 us -> 37.5 us
    all_gather x1 -> x0, blocking collectives: 277 us -> none  [local(): lax.all_gather(occ_column, 'wide', axis=0, tiled=True)]
    all_to_all x1, waiting for transfers between devices: 0.01 us -> 175 us  [local(): lax.all_to_all(outgoing.reshape(wide_count, CAP, block_size, wide_row), '...]
    all_to_all x0 -> x1, starting transfers between devices: none -> 20.6 us  [local(): lax.all_to_all(jnp.stack([occ_column] * lax.axis_size('wide')), 'wide', 0...]
  transfers between devices with their start and end apart: 2 -> 3, of which waited for: 1 -> 2; matrix products, arithmetic and copies ran while one was open for 1% -> 5% of each run, Pallas kernels for 0% -> 0%
where the time goes in v2:
time: 713 us; the launch traced here: 712 us
  waiting for transfers between devices  613 us (86%)
  starting transfers between devices  37.5 us (5%)
  local copies, waits for them, and re-layouts  34.6 us (5%)
  between operations  13.6 us (2%)
  other arithmetic  7.81 us (1%)
    psum x1, waiting for transfers between devices, local(): total = lax.psum(response_part, ('wide', 'pair'))  438 us
    all_to_all x1, waiting for transfers between devices, local(): lax.all_to_all(outgoing.reshape(wide_count, CAP, block_size, wide_row), '...  175 us
    all_to_all x1, starting transfers between devices, local(): lax.all_to_all(jnp.stack([occ_column] * lax.axis_size('wide')), 'wide', 0...  20.6 us
    all_to_all x1, starting transfers between devices, local(): lax.all_to_all(outgoing.reshape(wide_count, CAP, block_size, wide_row), '...  16.7 us
    scatter x1, local copies, waits for them, and re-layouts, local(): jnp.zeros((slot_total, block_size, wide_row), jnp.bfloat16).at[position]  15.7 us
  transfers between devices with their start and end apart: 3, of which 2 were waited for; matrix products, arithmetic and copies ran while one was open for 5% of the time, Pallas kernels for 0%

profile of v2, /device:TPU:1, one launch (start us, length us, event | category | flops | bytes accessed | tf_op | source)
XLA Modules:
  0.0 712.0 jit_solution(8486088965007823313)
XLA Ops:
  6.5 0.7 stack.2
  7.3 0.8 reshape.170
  8.1 20.6 %all-to-all-start = ((s32[128,1,128]{2,1,0:T(1,128)}), s32[128,1,128]{2,1,0:T(1,128)S(1)}, u32[]{:S(2)}, u32[]{:S(2)}) async-start(s32[128,1,128]{2,1,0:T(1,128)} %reshape.170), calls=%async_computation | async-start | bytes 131072 | tf_op jit(solution)/shard_map/all_to_all | solution.py:31
  28.6 0.7 broadcast_multiply_fusion
  29.3 0.1 eq.80
  29.4 1.1 copy.38
  30.5 1.1 copy.32
  31.6 0.7 convert_element_type.22
  32.3 1.5 multiply_convert_fusion
  33.9 2.0 convert_bitcast_fusion
  35.9 0.2 convert_reduce_fusion.1
  36.1 0.1 mul.26
  36.2 2.8 reshape.164
  39.0 2.5 broadcast_in_dim.12
  41.5 15.7 %scatter_fusion = bf16[256,8,1024]{2,1,0:T(8,128)(2,1)} fusion(bf16[256,8,1024]{2,1,0:T(8,128)(2,1)} %broadcast_in_dim.12, s32[128]{0:T(128)S(1)} %fusion.17, bf16[128,8,1024]{2,1,0:T(8,128)(2,1)S(1)} %reshape.164), kind=kCustom, calls=%fused_computation | custom fusion | bytes 6291968 | tf_op jit(solution)/shard_map/scatter | solution.py:51
  57.2 0.0 all-to-all-done
  57.2 0.0 copy-start
  57.2 16.7 %all-to-all-start.1 = ((bf16[128,2,8,1024]{3,2,1,0:T(8,128)(2,1)}), bf16[128,2,8,1024]{3,2,1,0:T(8,128)(2,1)}, u32[]{:S(2)}, u32[]{:S(2)}) async-start(bf16[128,2,8,1024]{3,2,1,0:T(8,128)(2,1)} %bitcast.57), calls=%async_computation.1 | async-start | bytes 8388608 | tf_op jit(solution)/shard_map/all_to_all | solution.py:52
  73.9 0.2 all-reduce.2.cloned.1.call-start
  74.2 0.0 copy-done
  74.2 0.5 broadcast.149
  74.8 0.8 reduce
  75.6 0.2 reshape.171
  75.7 0.1 copy.25
  75.9 0.1 copy.29
  76.0 0.1 broadcast_compare_fusion
  76.0 0.1 copy.27
  76.1 0.1 copy.26
  76.3 5.1 convert_reduce_fusion
  81.4 0.1 select_reduce_fusion
  81.5 0.1 copy.30
  81.6 0.1 eq.76
  81.8 0.1 fusion.5
  81.9 0.1 copy.31
  82.0 0.2 and.81
  82.2 175.3 %all-to-all-done.1 = bf16[128,2,8,1024]{3,2,1,0:T(8,128)(2,1)} async-done(((bf16[128,2,8,1024]{3,2,1,0:T(8,128)(2,1)}), bf16[128,2,8,1024]{3,2,1,0:T(8,128)(2,1)}, u32[]{:S(2)}, u32[]{:S(2)}) %all-to-all-start.1) | async-done | bytes 4194336 | tf_op jit(solution)/shard_map/all_to_all | solution.py:52
  257.4 6.5 copy.40
  264.0 0.7 fusion.11
  264.6 0.1 reshape.158
  264.7 0.9 fusion.18
  265.6 0.0 all-reduce.2.cloned.1.call-update
  265.7 438.2 %all-reduce.2.cloned.1.call-done = f32[128,128]{1,0:T(8,128)} async-done(((f32[128,128]{1,0:T(8,128)}), f32[128,128]{1,0:T(8,128)}) %all-reduce.2.cloned.1.call-update) | async-done | bytes 65552 | tf_op jit(solution)/shard_map/psum | solution.py:73
  703.8 1.3 constant_dynamic-slice_fusion
  (4 shorter events, 0.1 us)
Async XLA Ops:
  8.1 49.2 %all-to-all-start = ((s32[128,1,128]{2,1,0:T(1,128)}), s32[128,1,128]{2,1,0:T(1,128)S(1)}, u32[]{:S(2)}, u32[]{:S(2)}) async-start(s32[128,1,128]{2,1,0:T(1,128)} %reshape.170), calls=%async_computation | async-start | bytes 131072 | tf_op jit(solution)/shard_map/all_to_all | solution.py:31
  57.2 16.9 %copy-start = (bf16[4,8,1024]{2,1,0:T(8,128)(2,1)S(1)}, bf16[4,8,1024]{2,1,0:T(8,128)(2,1)}, u32[]{:S(2)}) copy-start(bf16[4,8,1024]{2,1,0:T(8,128)(2,1)} %param.5) | copy-start | bytes 196612
  57.2 200.2 %all-to-all-start.1 = ((bf16[128,2,8,1024]{3,2,1,0:T(8,128)(2,1)}), bf16[128,2,8,1024]{3,2,1,0:T(8,128)(2,1)}, u32[]{:S(2)}, u32[]{:S(2)}) async-start(bf16[128,2,8,1024]{3,2,1,0:T(8,128)(2,1)} %bitcast.57), calls=%async_computation.1 | async-start | bytes 8388608 | tf_op jit(solution)/shard_map/all_to_all | solution.py:52
  73.9 629.9 %all-reduce.2.cloned.1.call-start = ((), (), s32[]{:S(2)}) async-start(), calls=%async_computation.2 | async-start | bytes 131072 | tf_op jit(solution)/shard_map/psum | solution.py:73
Sparse Core Ops, SparseCore 0:
  265.8 438.0 all-reduce.1

commit v3 on v0

--- a/solution.py
+++ b/solution.py
@@ -68,7 +68,7 @@
         precision=lax.Precision.HIGHEST,
         preferred_element_type=jnp.float32,
     )
-    total = lax.psum(response_part, ("wide", "pair"))
+    total = jnp.sum(lax.all_gather(response_part, ("wide", "pair")), axis=0)
     row_count = aux_count // lax.axis_size("pair")
     result = lax.dynamic_slice_in_dim(total, lax.axis_index("pair") * row_count, row_count, 0)
     return result

time: 794 us -> 605 us (0.76)
  waiting for transfers between devices: 438 us -> 236 us
  other arithmetic: 7.01 us -> 20.1 us
    psum x1 -> x0, waiting for transfers between devices: 438 us -> none  [local(): total = lax.psum(response_part, ('wide', 'pair'))]
    all_gather x0 -> x1, waiting for transfers between devices: none -> 236 us  [local(): total = jnp.sum(lax.all_gather(response_part, ('wide', 'pair')), axis=0)]
    reduce_sum x0 -> x1, other arithmetic: none -> 13.1 us  [local(): total = jnp.sum(lax.all_gather(response_part, ('wide', 'pair')), axis=0)]
where the time goes in v3:
time: 605 us; the launch traced here: 604 us
  blocking collectives  276 us (46%)
  waiting for transfers between devices  236 us (39%)
  local copies, waits for them, and re-layouts  31.6 us (5%)
  starting transfers between devices  21.2 us (4%)
  other arithmetic  20.1 us (3%)
  between operations  13.6 us (2%)
    all_gather x1, blocking collectives, local(): lax.all_gather(occ_column, 'wide', axis=0, tiled=True)  276 us
    all_gather x1, waiting for transfers between devices, local(): total = jnp.sum(lax.all_gather(response_part, ('wide', 'pair')), axis=0)  236 us
    all_to_all x1, starting transfers between devices, local(): lax.all_to_all(outgoing.reshape(wide_count, CAP, block_size, wide_row), '...  21.1 us
    scatter x1, local copies, waits for them, and re-layouts, local(): jnp.zeros((slot_total, block_size, wide_row), jnp.bfloat16).at[position]  15.7 us
    reduce_sum x1, other arithmetic, local(): total = jnp.sum(lax.all_gather(response_part, ('wide', 'pair')), axis=0)  13.1 us
  transfers between devices with their start and end apart: 2, of which 1 were waited for; matrix products, arithmetic and copies ran while one was open for 1% of the time, Pallas kernels for 0%

profile of v3, /device:TPU:1, one launch (start us, length us, event | category | flops | bytes accessed | tf_op | source)
XLA Modules:
  0.0 603.8 jit_solution(11082680124360632235)
XLA Ops:
  6.5 0.7 convert_element_type.22
  7.2 0.7 broadcast_multiply_fusion
  7.9 0.1 mul.26
  8.0 0.1 eq.80
  8.1 0.2 convert_reduce_fusion.1
  8.3 1.1 copy.33
  9.4 1.1 copy.39
  10.5 1.5 multiply_convert_fusion
  12.0 2.0 convert_bitcast_fusion
  14.1 2.8 reshape.166
  16.9 2.5 broadcast_in_dim.12
  19.4 15.7 %scatter_fusion = bf16[256,8,1024]{2,1,0:T(8,128)(2,1)} fusion(bf16[256,8,1024]{2,1,0:T(8,128)(2,1)} %broadcast_in_dim.12, s32[128]{0:T(128)S(1)} %fusion.17, bf16[128,8,1024]{2,1,0:T(8,128)(2,1)S(1)} %reshape.166), kind=kCustom, calls=%fused_computation | custom fusion | bytes 6291968 | tf_op jit(solution)/shard_map/scatter | solution.py:49
  35.1 0.0 copy-start
  35.1 0.0 copy-start.1
  35.1 21.1 %all-to-all-start = ((bf16[128,2,8,1024]{3,2,1,0:T(8,128)(2,1)}), bf16[128,2,8,1024]{3,2,1,0:T(8,128)(2,1)}, u32[]{:S(2)}, u32[]{:S(2)}) async-start(bf16[128,2,8,1024]{3,2,1,0:T(8,128)(2,1)} %bitcast.61), calls=%async_computation | async-start | bytes 8388608 | tf_op jit(solution)/shard_map/all_to_all | solution.py:50
  56.3 0.0 all-gather.4.cloned.1.call-start
  56.3 0.0 copy-done
  56.4 0.0 copy-done.1
  56.4 276.5 %all-gather.1 = s32[128,4,32]{2,1,0:T(4,128)S(1)} all-gather(s32[1,4,32]{2,1,0:T(4,128)S(1)} %bitcast.65), channel_id=1, replica_groups=mesh['wide'=128,'pair'=4] {'wide'}, dimensions={0}, use_global_device_ids=true | all-gather | bytes 66048 | tf_op jit(solution)/shard_map/all_gather | solution.py:30
  332.9 0.1 copy.26
  333.1 0.1 copy.30
  333.2 0.1 broadcast_compare_fusion
  333.2 0.1 copy.27
  333.3 0.1 copy.28
  333.5 5.1 convert_reduce_fusion
  338.6 0.1 fusion.5
  338.7 0.1 copy.32
  338.8 0.2 and.81
  339.0 0.1 select_reduce_fusion
  339.1 0.1 copy.31
  339.2 0.1 eq.76
  339.4 0.0 all-to-all-done
  339.4 6.5 %copy.41 = bf16[32,8,8,1024]{3,1,2,0:T(8,128)(2,1)S(1)} copy(bf16[32,8,8,1024]{3,2,1,0:T(8,128)(2,1)} %bitcast.18) | data formatting | bytes 8388608
  345.9 0.7 fusion.11
  346.6 0.1 reshape.160
  346.7 0.9 fusion.18
  347.6 0.0 all-gather.4.cloned.1.call-update
  347.6 235.7 %all-gather.4.cloned.1.call-done = f32[65536,128]{1,0:T(8,128)} async-done(((f32[128,128]{1,0:T(8,128)}), f32[65536,128]{1,0:T(8,128)}) %all-gather.4.cloned.1.call-update) | async-done | bytes 33554448 | tf_op jit(solution)/shard_map/all_gather | solution.py:71
  583.3 13.1 %reduce_sum.42 = f32[128,128]{1,0:T(8,128)S(1)} reduce(f32[512,128,128]{2,1,0:T(8,128)} %bitcast.60, f32[]{:T(128)} %constant.57.clone.1), dimensions={0}, to_apply=%region_5.6 | reduce | flops 8372224 | bytes 33619972 | tf_op jit(solution)/shard_map/reduce_sum | solution.py:71
  596.4 0.6 constant_dynamic-slice_fusion
  (4 shorter events, 0.1 us)
Async XLA Ops:
  35.1 21.2 %copy-start = (bf16[4,8,1024]{2,1,0:T(8,128)(2,1)S(1)}, bf16[4,8,1024]{2,1,0:T(8,128)(2,1)}, u32[]{:S(2)}) copy-start(bf16[4,8,1024]{2,1,0:T(8,128)(2,1)} %param.5) | copy-start | bytes 196612
  35.1 21.3 %copy-start.1 = (s32[4,32]{1,0:T(4,128)S(1)}, s32[4,32]{1,0:T(4,128)}, u32[]{:S(2)}) copy-start(s32[4,32]{1,0:T(4,128)} %param.8) | copy-start | bytes 1540
  35.1 304.2 %all-to-all-start = ((bf16[128,2,8,1024]{3,2,1,0:T(8,128)(2,1)}), bf16[128,2,8,1024]{3,2,1,0:T(8,128)(2,1)}, u32[]{:S(2)}, u32[]{:S(2)}) async-start(bf16[128,2,8,1024]{3,2,1,0:T(8,128)(2,1)} %bitcast.61), calls=%async_computation | async-start | bytes 8388608 | tf_op jit(solution)/shard_map/all_to_all | solution.py:50
  56.3 527.0 %all-gather.4.cloned.1.call-start = ((), (), s32[]{:S(2)}) async-start(), calls=%async_computation.1 | async-start | bytes 33619968 | tf_op jit(solution)/shard_map/all_gather | solution.py:71
Sparse Core Ops, SparseCore 0:
  347.7 235.5 all-gather.3
